TPU v7x, 32 devices: a whole 2x2x4 slice. The times are simulated.
32 devices in a mesh: section: 2 (over x), dp: 16 (over z, y, core).
Axes of the slice: x: 2, y: 2, z: 4, core: 2. Of those that a mesh axis runs over, the one named last changes fastest.
Arguments:
- tokens_in: bfloat16 [3, 1024, 1024], P(None, 'dp'), may hold values from -6 to 6
- out_cotangent: bfloat16 [3, 1024, 1024], P(None, 'dp'), may hold values from -6 to 6
- in_weight: bfloat16 [2, 1024, 4384], P('section', 'dp'), may hold values from -0.1875 to 0.1875
- out_weight: bfloat16 [2, 2048, 1024], P('section', 'dp'), may hold values from -0.125 to 0.125
- norm_gain: float32 [2, 1024], P('section'), may hold values from 0.5 to 1.5
- conv_weight: float32 [2, 4, 2304], P('section'), may hold values from -3 to 3
- conv_bias: float32 [2, 2304], P('section'), may hold values from -3 to 3
- dt_bias: float32 [2, 32], P('section'), may hold values from -4 to 0
- a_log: float32 [2, 32], P('section'), may hold values from 0 to 2.77
- skip_gain: float32 [2, 32], P('section'), may hold values from 0.5 to 1.5
- gate_gain: float32 [2, 2048], P('section'), may hold values from 0.5 to 1.5
- group_fill: int32 [3, 32], P(None, 'dp'), may hold values from 0 to 32, as said below
- group_link: int32 [3, 32], P(None, 'dp'), may hold values from 0 to 1, as said below
Outputs:
- section_outputs: float32 [2, 3, 1024, 1024], P('section', None, 'dp')
- section_input_grads: float32 [2, 3, 1024, 1024], P('section', None, 'dp')
- grad_in_weight: float32 [2, 1024, 4384], P('section', 'dp')
- grad_out_weight: float32 [2, 2048, 1024], P('section', 'dp')
- grad_norm_gain: float32 [2, 1024], P('section')
- grad_conv_weight: float32 [2, 4, 2304], P('section')
- grad_conv_bias: float32 [2, 2304], P('section')
- grad_dt_bias: float32 [2, 32], P('section')
- grad_a_log: float32 [2, 32], P('section')
- grad_skip_gain: float32 [2, 32], P('section')
- grad_gate_gain: float32 [2, 2048], P('section')
Inputs may be any that keep to these rules, and one draw needn't show every extreme that they name: `group_fill`: each slot's groups hold whole sequences from the start of a group: a sequence fills groups, the last one from its start to its end, the rest of that group is unused; some groups are empty, and how many differs from slot to slot. Some group of every micro-batch is full. `group_link`: A link of 1 stands only on a group that is not the first of its slot, follows a full group and holds a token; every micro-batch has one.
All inputs are finite; a program needn't handle non-finite values.
Results may differ from a plain program's by a relative error of at most 0.0097.
Values may be sent and summed in bfloat16 or wider, within the bound.
No kernel may reach another device: no remote copies, remote signals or barrier semaphores. Data moves between devices by JAX's collectives and lax.ppermute only.
A program may use at most 128 MiB of HBM per device.

v0:
```python
import jax
import jax.numpy as jnp
from jax import lax
from jax.sharding import PartitionSpec as P

EPSILON = 1e-05
HIGHEST = lax.Precision.HIGHEST


def shifted_2(x, axis, by):
    peers = lax.axis_size(axis)
    pairs = [(i, i + by) for i in range(peers) if 0 <= i + by < peers]
    return lax.ppermute(x, axis, pairs)


def norm_map(values, gain_row):
    return (
        values * lax.rsqrt(jnp.mean(values * values, axis=-1, keepdims=True) + EPSILON) * gain_row
    )


def ssd_scan(x_heads, step_size, log_decay, input_b, input_c, link_row, groups):
    rows_all, head_count, head_size = x_heads.shape
    length = rows_all // groups
    state_size = input_b.shape[1]
    x_blocks = x_heads.reshape(groups, length, head_count, head_size)
    dt_blocks = step_size.reshape(groups, length, head_count)
    cumulative = jnp.cumsum(log_decay.reshape(groups, length, head_count), axis=1)
    b_blocks = input_b.reshape(groups, length, state_size)
    c_blocks = input_c.reshape(groups, length, state_size)
    scores = jnp.einsum("cin,cjn->cij", c_blocks, b_blocks, precision=HIGHEST)
    causal = jnp.arange(length)[:, None] >= jnp.arange(length)[None, :]
    decay_gap = cumulative[:, :, None, :] - cumulative[:, None, :, :]
    factors = jnp.exp(jnp.where(causal[None, :, :, None], decay_gap, -jnp.inf))
    factors = factors * scores[..., None] * dt_blocks[:, None, :, :]
    diag_out = jnp.einsum("cijh,cjhp->cihp", factors, x_blocks, precision=HIGHEST)
    group_end = cumulative[:, -1:, :]
    to_end = jnp.exp(group_end - cumulative) * dt_blocks
    group_states = jnp.einsum("cjh,cjhp,cjn->chpn", to_end, x_blocks, b_blocks, precision=HIGHEST)
    group_decay = jnp.exp(group_end[:, 0, :])
    link_float = link_row.astype(jnp.float32)
    carried = jnp.zeros((head_count, head_size, state_size), jnp.float32)
    entering = [carried]
    carried = link_float[1] * (group_decay[0][:, None, None] * carried + group_states[0])
    entering.append(carried)
    entering = jnp.stack(entering)
    off_out = jnp.einsum(
        "cih,cin,chpn->cihp", jnp.exp(cumulative), c_blocks, entering, precision=HIGHEST
    )
    return (diag_out + off_out).reshape(rows_all, head_count, head_size)


def mixer_slot(
    projected, conv_weight, conv_bias, dt_bias, a_log, skip_gain, gate_gain, fill_row, link_row
):
    rows_all = projected.shape[0]
    groups = fill_row.shape[0]
    length = rows_all // groups
    inner_size = gate_gain.shape[0]
    head_count = dt_bias.shape[0]
    conv_size = conv_bias.shape[0]
    state_size = (conv_size - inner_size) // 2
    head_size = inner_size // head_count
    gate_part = projected[:, :inner_size]
    conv_in = projected[:, inner_size : inner_size + conv_size]
    dt_raw = projected[:, inner_size + conv_size :]
    within = jnp.arange(rows_all) % length
    linked = jnp.broadcast_to(link_row.astype(jnp.float32)[:, None], (groups, length)).reshape(
        rows_all
    )
    filled = jnp.broadcast_to(fill_row[:, None], (groups, length)).reshape(rows_all)
    valid = (within < filled).astype(jnp.float32)
    conv_sum = conv_bias + conv_weight[0] * conv_in
    for lag_steps in range(1, conv_weight.shape[0]):
        shifted = jnp.concatenate(
            [jnp.zeros((lag_steps, conv_size), jnp.float32), conv_in[:-lag_steps]], axis=0
        )
        keep_mask = jnp.maximum((within >= lag_steps).astype(jnp.float32), linked)
        conv_sum = conv_sum + conv_weight[lag_steps] * shifted * keep_mask[:, None]
    activated = jax.nn.silu(conv_sum)
    x_heads = activated[:, :inner_size].reshape(rows_all, head_count, head_size)
    input_b = activated[:, inner_size : inner_size + state_size]
    input_c = activated[:, inner_size + state_size :]
    step_size = jax.nn.softplus(dt_raw + dt_bias)
    log_decay = step_size * -jnp.exp(a_log)
    scanned = ssd_scan(x_heads, step_size, log_decay, input_b, input_c, link_row, groups)
    scanned = scanned + skip_gain[:, None] * x_heads
    gated = scanned.reshape(rows_all, inner_size) * jax.nn.silu(gate_part)
    return norm_map(gated, gate_gain) * valid[:, None]


def outer_term(left_rows, right_rows):
    return lax.dot_general(
        left_rows, right_rows, (((0,), (0,)), ((), ())), preferred_element_type=jnp.float32
    )


def on_device(
    tokens_in,
    out_cotangent,
    in_weight,
    out_weight,
    norm_gain,
    conv_weight,
    conv_bias,
    dt_bias,
    a_log,
    skip_gain,
    gate_gain,
    group_fill,
    group_link,
):
    contract_cols = (((1,), (1,)), ((), ()))
    micro_count = tokens_in.shape[0]
    section_count = lax.axis_size("section")
    section_index = lax.axis_index("section")
    is_first = section_index == 0
    is_last = section_index == section_count - 1
    tick_count = micro_count + section_count - 1
    params = (conv_weight[0], conv_bias[0], dt_bias[0], a_log[0], skip_gain[0], gate_gain[0])
    gain_row = norm_gain[0]
    full_in, full_out = (
        lax.all_gather(in_weight, "dp", axis=1, tiled=True),
        lax.all_gather(out_weight, "dp", axis=1, tiled=True),
    )
    weight_in = full_in[0]
    weight_out = full_out[0]
    tick_list = jnp.arange(tick_count, dtype=jnp.int32)

    def forward_tick(received, tick_index):
        batch_index = jnp.clip(tick_index - section_index, 0, micro_count - 1)
        own_rows = lax.dynamic_index_in_dim(
            tokens_in, jnp.minimum(tick_index, micro_count - 1), 0, keepdims=False
        )
        layer_in = jnp.where(is_first, own_rows, received)
        fill_row = lax.dynamic_index_in_dim(group_fill, batch_index, 0, keepdims=False)
        link_row = lax.dynamic_index_in_dim(group_link, batch_index, 0, keepdims=False)
        residual = layer_in.astype(jnp.float32)
        normed = norm_map(residual, gain_row).astype(jnp.bfloat16)
        projected = jnp.dot(normed, weight_in, preferred_element_type=jnp.float32)
        mixed = mixer_slot(projected, *params, fill_row, link_row).astype(jnp.bfloat16)
        output = residual + jnp.dot(mixed, weight_out, preferred_element_type=jnp.float32)
        sent = shifted_2(output.astype(jnp.bfloat16), "section", 1)
        return (sent, (layer_in, normed, projected, mixed, output))

    start_rows = jnp.zeros(tokens_in.shape[1:], jnp.bfloat16)
    unused_rows, kept = lax.scan(forward_tick, start_rows, tick_list)
    stack_inputs, stack_normed, stack_projected, stack_mixed, stack_outputs = kept
    section_outputs = lax.dynamic_slice_in_dim(stack_outputs, section_index, micro_count, 0)[None]
    again_in, again_out = (
        lax.all_gather(in_weight, "dp", axis=1, tiled=True),
        lax.all_gather(out_weight, "dp", axis=1, tiled=True),
    )
    weight_in = again_in[0]
    weight_out = again_out[0]

    def backward_tick(carry, tick_index):
        back_received, small_sums, shard_in, shard_out = carry
        saved_index = jnp.clip(
            tick_index - section_count + 1 + 2 * section_index, 0, tick_count - 1
        )
        batch_index = jnp.clip(tick_index - section_count + 1 + section_index, 0, micro_count - 1)
        own_grad = lax.dynamic_index_in_dim(
            out_cotangent, jnp.minimum(tick_index, micro_count - 1), 0, keepdims=False
        ).astype(jnp.float32)
        own_grad = jnp.where(tick_index < micro_count, own_grad, jnp.zeros_like(own_grad))
        upstream = jnp.where(is_last, own_grad, back_received.astype(jnp.float32))
        fill_row = lax.dynamic_index_in_dim(group_fill, batch_index, 0, keepdims=False)
        link_row = lax.dynamic_index_in_dim(group_link, batch_index, 0, keepdims=False)
        residual = lax.dynamic_index_in_dim(stack_inputs, saved_index, 0, keepdims=False).astype(
            jnp.float32
        )
        normed = lax.dynamic_index_in_dim(stack_normed, saved_index, 0, keepdims=False)
        projected = lax.dynamic_index_in_dim(stack_projected, saved_index, 0, keepdims=False)
        mixed = lax.dynamic_index_in_dim(stack_mixed, saved_index, 0, keepdims=False)
        upper_lower = upstream.astype(jnp.bfloat16)
        d_mixed = lax.dot_general(
            upper_lower, weight_out, contract_cols, preferred_element_type=jnp.float32
        )

        def local_map(proj_rows, *param_list):
            return mixer_slot(proj_rows, *param_list, fill_row, link_row)

        unused, pull_back = jax.vjp(local_map, projected, *params)
        pulled = pull_back(d_mixed)
        d_low = pulled[0].astype(jnp.bfloat16)
        d_normed = lax.dot_general(
            d_low, weight_in, contract_cols, preferred_element_type=jnp.float32
        )
        unused_norm, pull_norm = jax.vjp(norm_map, residual, gain_row)
        d_residual, d_gain = pull_norm(d_normed)
        input_grad = upstream + d_residual
        tick_small = (d_gain,) + tuple(pulled[1:])
        small_sums = jax.tree.map(jnp.add, small_sums, tick_small)
        sent_back = shifted_2(input_grad.astype(jnp.bfloat16), "section", -1)
        return (
            (sent_back, small_sums, shard_in, shard_out),
            (normed, d_low, mixed, upper_lower, input_grad),
        )

    small_start = jax.tree.map(
        lambda item: jnp.zeros(item.shape, jnp.float32), (gain_row,) + params
    )
    shard_start_in = jnp.zeros(in_weight.shape[1:], jnp.float32)
    shard_start_out = jnp.zeros(out_weight.shape[1:], jnp.float32)
    carry_start = (start_rows, small_start, shard_start_in, shard_start_out)
    carry_end, tick_outputs = lax.scan(backward_tick, carry_start, tick_list)
    unused_back, small_sums, shard_in, shard_out = carry_end
    list_normed, list_dproj, list_mixed, list_uplow, list_grads = tick_outputs
    all_normed = list_normed.reshape(-1, list_normed.shape[-1])
    all_dproj = list_dproj.reshape(-1, list_dproj.shape[-1])
    all_mixed = list_mixed.reshape(-1, list_mixed.shape[-1])
    all_uplow = list_uplow.reshape(-1, list_uplow.shape[-1])
    shard_in = lax.psum_scatter(
        outer_term(all_normed, all_dproj), "dp", scatter_dimension=0, tiled=True
    )
    shard_out = lax.psum_scatter(
        outer_term(all_mixed, all_uplow), "dp", scatter_dimension=0, tiled=True
    )
    summed = lax.psum(small_sums, "dp")
    section_input_grads = lax.dynamic_slice_in_dim(
        list_grads, section_count - 1 - section_index, micro_count, 0
    )[None]
    return (section_outputs, section_input_grads, shard_in[None], shard_out[None]) + tuple(
        (summed_grad[None] for summed_grad in summed)
    )


def solution(mesh):
    in_specs = (
        P(None, "dp", None),
        P(None, "dp", None),
        P("section", "dp", None),
        P("section", "dp", None),
        P("section", None),
        P("section", None, None),
        P("section", None),
        P("section", None),
        P("section", None),
        P("section", None),
        P("section", None),
        P(None, "dp"),
        P(None, "dp"),
    )
    out_specs = (
        P("section", None, "dp", None),
        P("section", None, "dp", None),
        P("section", "dp", None),
        P("section", "dp", None),
        P("section", None),
        P("section", None, None),
        P("section", None),
        P("section", None),
        P("section", None),
        P("section", None),
        P("section", None),
    )
    return jax.shard_map(
        on_device, mesh=mesh, in_specs=in_specs, out_specs=out_specs, check_vma=False
    )
```

profile of v0, /device:TPU:0, one launch (start us, length us, event | category | flops | bytes accessed | tf_op | source)
XLA Modules:
  0.0 1077.1 jit_solution(11850100364788017831)
XLA Ops:
  12.7 50.6 %all-gather.5.cloned.1.call-done = bf16[1,2048,1024]{2,1,0:T(8,128)(2,1)} async-done(((bf16[1,128,1024]{2,1,0:T(8,128)(2,1)}), bf16[1,2048,1024]{2,1,0:T(8,128)(2,1)}) %all-gather.5.cloned.1.call-update) | async-done | bytes 4194320 | tf_op jit(solution)/shard_map/all_gather | solution.py:124
  63.3 80.1 %all-gather.3.cloned.1.call-done = bf16[1,1024,4384]{2,1,0:T(8,128)(2,1)} async-done(((bf16[1,64,4384]{2,1,0:T(8,128)(2,1)}), bf16[1,1024,4384]{2,1,0:T(8,128)(2,1)}) %all-gather.3.cloned.1.call-update) | async-done | bytes 8978448 | tf_op jit(solution)/shard_map/all_gather | solution.py:123
  147.9 184.0 %while.61 = (s32[]{:T(128)}, bf16[64,1024]{1,0:T(8,128)(2,1)S(1)}, bf16[4,64,1024]{2,1,0:T(8,128)(2,1)}, bf16[4,64,1024]{2,1,0:T(8,128)(2,1)}, f32[4,64,4384]{2,...) while((s32[]{:T(128)}, bf16[64,1024]{1,0:T(8,128)(2,1)S(1)}, ...), condition=%wide.region_4.5_spmd, body=%wide.region_0.4_spmd.sunk | while | flops 1205211648 | bytes 37663164 | solution.py:147
  153.6 6.4 bitcast_dynamic-update-slice_fusion.17
  199.3 6.4 bitcast_dynamic-update-slice_fusion.17
  232.8 4.4 collective-permute-start
  245.4 6.4 bitcast_dynamic-update-slice_fusion.17
  279.0 4.4 collective-permute-start
  291.5 6.4 bitcast_dynamic-update-slice_fusion.17
  325.0 4.4 collective-permute-start
  336.5 430.2 %while.62 = (s32[]{:T(128)}, bf16[64,1024]{1,0:T(8,128)(2,1)S(1)}, f32[1024]{0:T(1024)}, f32[4,2304]{1,0:T(4,128)}, f32[2304]{0:T(1024)}, /*index=5*/f32[32]{0:T...) while((s32[]{:T(128)}, bf16[64,1024]{1,0:T(8,128)(2,1)S(1)}, ...), condition=%wide.region_29.30_spmd.clone, body=%wide.region_5.29_spmd.clone.sunk | while | flops 1929479168 | bytes 110034496 | solution.py:207
  392.4 4.4 multiply_reduce_fusion.25
  405.0 4.1 fusion.300
  409.2 3.9 multiply_reduce_fusion.27
  444.0 6.7 fusion.305
  494.8 4.4 multiply_reduce_fusion.25
  507.3 4.1 fusion.300
  511.5 3.9 multiply_reduce_fusion.27
  546.3 6.7 fusion.305
  597.1 4.4 multiply_reduce_fusion.25
  609.7 4.1 fusion.300
  613.8 3.9 multiply_reduce_fusion.27
  648.6 6.7 fusion.305
  699.5 4.4 multiply_reduce_fusion.25
  712.0 4.1 fusion.300
  716.2 3.9 multiply_reduce_fusion.27
  751.0 6.7 fusion.305
  766.7 6.0 convolution_bitcast_fusion.6
  774.5 8.9 convolution_bitcast_fusion.5
  784.3 61.2 %all-reduce.24 = (f32[1,1024]{1,0:T(1,128)}, f32[1,4,2304]{2,1,0:T(4,128)}, f32[1,2304]{1,0:T(1,128)}, f32[1,32]{1,0:T(1,128)}, f32[1,32]{1,0:T(1,128)}, /*index=5*/f32[1,32]{1,0:T(1,128)}, f32[1,2048]{1,0:T(1,128)}) all-reduce(f32[1,1024]{1,0:T(1,128)S(1)} %bitcast.403, ...), channel_id=1, replica_groups=mesh['section'=2,'dp'=16] {'dp'}, use_global_device_ids=true, to_apply=%region_32.33 | all-reduce | flops 14688 | bytes 117504 | tf_op jit(solution)/shard_map/psum | solution.py:220
  846.8 29.4 %reduce-scatter.5.cloned.1.call-done = f32[128,1024]{1,0:T(8,128)} async-done(((f32[2048,1024]{1,0:T(8,128)}), f32[128,1024]{1,0:T(8,128)}) %reduce-scatter.5.cloned.1.call-update) | async-done | bytes 524304 | tf_op jit(solution)/shard_map/reduce_scatter | solution.py:217
  876.1 194.0 %reduce-scatter.3.cloned.1.call-done = f32[64,4384]{1,0:T(8,128)} async-done(((f32[1024,4384]{1,0:T(8,128)}), f32[64,4384]{1,0:T(8,128)}) %reduce-scatter.3.cloned.1.call-update) | async-done | bytes 1122320 | tf_op jit(solution)/shard_map/reduce_scatter | solution.py:214
  (1357 shorter events, 477.8 us)
Async XLA Ops:
  7.2 140.7 %copy-start.28 = (f32[1,2048]{1,0:T(1,128)S(1)}, f32[1,2048]{1,0:T(1,128)}, u32[]{:S(2)}) copy-start(f32[1,2048]{1,0:T(1,128)} %param.27) | copy-start | bytes 24580
  7.2 140.7 %copy-start.27 = (f32[1,1024]{1,0:T(1,128)S(1)}, f32[1,1024]{1,0:T(1,128)}, u32[]{:S(2)}) copy-start(f32[1,1024]{1,0:T(1,128)} %param.21) | copy-start | bytes 12292
  7.2 56.1 %all-gather.5.cloned.1.call-start = ((), (), s32[]{:S(2)}) async-start(), calls=%async_computation.3 | async-start | bytes 4456448 | tf_op jit(solution)/shard_map/all_gather | solution.py:124
  7.9 135.4 %all-gather.3.cloned.1.call-start = ((), (), s32[]{:S(2)}) async-start(), calls=%async_computation.2 | async-start | bytes 9748480 | tf_op jit(solution)/shard_map/all_gather | solution.py:123
  8.7 867.4 %reduce-scatter.5.cloned.1.call-start = ((), (), s32[]{:S(2)}) async-start(), calls=%async_computation.5 | async-start | bytes 8912896 | tf_op jit(solution)/shard_map/reduce_scatter | solution.py:217
  187.1 6.5 collective-permute-start
  232.8 6.9 collective-permute-start
  279.0 6.9 collective-permute-start
  325.0 6.9 collective-permute-start
  357.2 35.3 %copy-start.12 = (bf16[64,1024]{1,0:T(8,128)(2,1)}, bf16[64,1024]{1,0:T(8,128)(2,1)S(1)}, u32[]{:S(2)}) copy-start(bf16[64,1024]{1,0:T(8,128)(2,1)S(1)} %get-tuple-element.2087) | copy-start | bytes 393220 | tf_op jit(solution)/shard_map/while
  443.9 10.1 copy-start.55
  444.0 10.2 copy-start.58
  452.5 6.8 collective-permute-start.1
  459.5 35.3 %copy-start.12 = (bf16[64,1024]{1,0:T(8,128)(2,1)}, bf16[64,1024]{1,0:T(8,128)(2,1)S(1)}, u32[]{:S(2)}) copy-start(bf16[64,1024]{1,0:T(8,128)(2,1)S(1)} %get-tuple-element.2087) | copy-start | bytes 393220 | tf_op jit(solution)/shard_map/while
  546.2 10.1 copy-start.54
  546.3 10.1 copy-start.56
  546.3 10.2 copy-start.55
  546.3 10.2 copy-start.58
  554.9 6.8 collective-permute-start.1
  561.8 35.3 %copy-start.12 = (bf16[64,1024]{1,0:T(8,128)(2,1)}, bf16[64,1024]{1,0:T(8,128)(2,1)S(1)}, u32[]{:S(2)}) copy-start(bf16[64,1024]{1,0:T(8,128)(2,1)S(1)} %get-tuple-element.2087) | copy-start | bytes 393220 | tf_op jit(solution)/shard_map/while
  648.6 10.1 copy-start.54
  648.6 10.1 copy-start.56
  648.6 10.2 copy-start.55
  648.6 10.2 copy-start.58
  657.2 6.8 collective-permute-start.1
  664.2 35.3 %copy-start.12 = (bf16[64,1024]{1,0:T(8,128)(2,1)}, bf16[64,1024]{1,0:T(8,128)(2,1)S(1)}, u32[]{:S(2)}) copy-start(bf16[64,1024]{1,0:T(8,128)(2,1)S(1)} %get-tuple-element.2087) | copy-start | bytes 393220 | tf_op jit(solution)/shard_map/while
  751.0 10.1 copy-start.55
  751.0 10.2 copy-start.58
  759.6 6.8 collective-permute-start.1
  772.7 297.4 %reduce-scatter.3.cloned.1.call-start = ((), (), s32[]{:S(2)}) async-start(), calls=%async_computation.4 | async-start | bytes 19496960 | tf_op jit(solution)/shard_map/reduce_scatter | solution.py:214
  783.5 62.0 %copy-start.43 = (f32[4,64,1024]{2,1,0:T(8,128)S(1)}, f32[4,64,1024]{2,1,0:T(8,128)}, u32[]{:S(2)}) copy-start(f32[4,64,1024]{2,1,0:T(8,128)} %get-tuple-element.969) | copy-start | bytes 3145732
  783.5 62.0 %copy-start.44 = (f32[4,64,1024]{2,1,0:T(8,128)S(1)}, f32[4,64,1024]{2,1,0:T(8,128)}, u32[]{:S(2)}) copy-start(f32[4,64,1024]{2,1,0:T(8,128)} %get-tuple-element.964) | copy-start | bytes 3145732
  (357 other events, 1691.6 us)
Sparse Core Ops, SparseCore 0:
  10.2 53.0 all-gather.4
  65.6 77.7 all-gather.2
  772.9 103.2 reduce-scatter.4
  880.8 189.3 reduce-scatter.2
where the time goes:
time: 1090 us; the launch traced here: 1080 us
  waiting for transfers between devices  360 us (33%)
  matrix products  249 us (23%)
  local copies, waits for them, and re-layouts  170 us (16%)
  other arithmetic  161 us (15%)
  blocking collectives  61.2 us (6%)
  loops' own time  39.4 us (4%)
  starting transfers between devices  21.8 us (2%)
  between operations  14.3 us (1%)
    reduce_scatter x1, waiting for transfers between devices, on_device(): lax.psum_scatter(outer_term(all_normed, all_dproj), 'dp', scatter_dimensi...  194 us
    all_gather x1, waiting for transfers between devices, on_device(): lax.all_gather(in_weight, 'dp', axis=1, tiled=True)  80.1 us
    psum x1, blocking collectives, on_device(): summed = lax.psum(small_sums, 'dp')  61.2 us
    all_gather x1, waiting for transfers between devices, on_device(): lax.all_gather(out_weight, 'dp', axis=1, tiled=True)  50.6 us
    dot_general x16, matrix products, ssd_scan(): jnp.einsum('cijh,cjhp->cihp', factors, x_blocks, precision=HIGHEST)  48.8 us
    another operation x1, loops' own time, on_device(): carry_end, tick_outputs = lax.scan(backward_tick, carry_start, tick_list)  33.3 us
    dot_general x12, matrix products, ssd_scan(): jnp.einsum('cih,cin,chpn->cihp', jnp.exp(cumulative), c_blocks, entering,...  31.7 us
    reduce_scatter x1, waiting for transfers between devices, on_device(): lax.psum_scatter(outer_term(all_mixed, all_uplow), 'dp', scatter_dimensio...  29.4 us
  transfers between devices with their start and end apart: 12, of which 12 were waited for; matrix products, arithmetic and copies ran while one was open for 4% of the time, Pallas kernels for 0%

commit v1 on v0

--- a/solution.py
+++ b/solution.py
@@ -5,6 +5,19 @@
 
 EPSILON = 1e-05
 HIGHEST = lax.Precision.HIGHEST
+
+
+def collect(x, axis, dim):
+    ways = lax.axis_size(axis)
+    up = [(d, (d + 1) % ways) for d in range(ways)]
+    down = [(d, (d - 1) % ways) for d in range(ways)]
+    earlier, later = ([x], [x])
+    for _ in range(ways // 2):
+        earlier.append(lax.ppermute(earlier[-1], axis, up))
+    for _ in range((ways - 1) // 2):
+        later.append(lax.ppermute(later[-1], axis, down))
+    line = jnp.concatenate([*earlier[::-1], *later[1:]], axis=dim)
+    return jnp.roll(line, (lax.axis_index(axis) - ways // 2) * x.shape[dim], axis=dim)
 
 
 def shifted_2(x, axis, by):
@@ -120,7 +133,7 @@
     params = (conv_weight[0], conv_bias[0], dt_bias[0], a_log[0], skip_gain[0], gate_gain[0])
     gain_row = norm_gain[0]
     full_in, full_out = (
-        lax.all_gather(in_weight, "dp", axis=1, tiled=True),
+        collect(in_weight, "dp", 1),
         lax.all_gather(out_weight, "dp", axis=1, tiled=True),
     )
     weight_in = full_in[0]

time: 1090 us -> 1250 us (1.15)
  local copies, waits for them, and re-layouts: 170 us -> 254 us
  waiting for transfers between devices: 360 us -> 312 us
  other arithmetic: 161 us -> 207 us
  starting transfers between devices: 21.8 us -> 56.3 us
  matrix products: 249 us -> 279 us
    all_gather x1, waiting for transfers between devices: 80.1 us -> 0.01 us  [on_device(): lax.all_gather(in_weight, 'dp', axis=1, tiled=True)]
    ppermute x0 -> x15, waiting for transfers between devices: none -> 79 us  [the longest x8 76.9 us: collect(): earlier.append(lax.ppermute(earlier[-1], axis, up))]
    all_gather x1, waiting for transfers between devices: 50.6 us -> 0.01 us  [on_device(): lax.all_gather(out_weight, 'dp', axis=1, tiled=True)]
    unnamed x26 -> x77, local copies, waits for them, and re-layouts: 2.49 us -> 43.3 us
    ppermute x0 -> x15, starting transfers between devices: none -> 34.1 us  [the longest x7 32.7 us: collect(): later.append(lax.ppermute(later[-1], axis, down))]
    add x24, other arithmetic: 0.44 us -> 23.8 us  [backward_tick(): small_sums = jax.tree.map(jnp.add, small_sums, tick_small)]
  transfers between devices with their start and end apart: 12 -> 27, of which waited for: 12 -> 16; matrix products, arithmetic and copies ran while one was open for 4% -> 23% of each run, Pallas kernels for 0% -> 0%
where the time goes in v1:
time: 1250 us; the launch traced here: 1230 us
  waiting for transfers between devices  312 us (25%)
  matrix products  279 us (22%)
  local copies, waits for them, and re-layouts  254 us (20%)
  other arithmetic  207 us (17%)
  blocking collectives  73.1 us (6%)
  starting transfers between devices  56.3 us (5%)
  loops' own time  36.6 us (3%)
  between operations  14.5 us (1%)
    reduce_scatter x1, waiting for transfers between devices, on_device(): lax.psum_scatter(outer_term(all_normed, all_dproj), 'dp', scatter_dimensi...  194 us
    ppermute x8, waiting for transfers between devices, collect(): earlier.append(lax.ppermute(earlier[-1], axis, up))  76.9 us
    psum x1, blocking collectives, on_device(): summed = lax.psum(small_sums, 'dp')  73.1 us
    dot_general x16, matrix products, ssd_scan(): jnp.einsum('cijh,cjhp->cihp', factors, x_blocks, precision=HIGHEST)  54.8 us
    unnamed x77, local copies, waits for them, and re-layouts  43.3 us
    dot_general x12, matrix products, ssd_scan(): jnp.einsum('cih,cin,chpn->cihp', jnp.exp(cumulative), c_blocks, entering,...  39.6 us
    reduce_scatter x1, waiting for transfers between devices, on_device(): lax.psum_scatter(outer_term(all_mixed, all_uplow), 'dp', scatter_dimensio...  37.7 us
    ppermute x7, starting transfers between devices, collect(): later.append(lax.ppermute(later[-1], axis, down))  32.7 us
  transfers between devices with their start and end apart: 27, of which 16 were waited for; matrix products, arithmetic and copies ran while one was open for 23% of the time, Pallas kernels for 0%

profile of v1, /device:TPU:0, one launch (start us, length us, event | category | flops | bytes accessed | tf_op | source)
XLA Modules:
  0.0 1232.8 jit_solution(1844961109799457680)
XLA Ops:
  8.5 12.6 %collective-permute-done.2 = bf16[1,64,4384]{2,1,0:T(8,128)(2,1)S(1)} collective-permute-done((bf16[1,64,4384]{2,1,0:T(8,128)(2,1)}, bf16[1,64,4384]{2,1,0:T(8,128)(2,1)S(1)}, u32[]{:S(2)}, u32[]{:S(2)}) %collective-permute-start.2) | collective-permute-done | bytes 561184 | tf_op jit(solution)/shard_map/ppermute | solution.py:16
  25.5 15.5 %collective-permute-done.3 = bf16[1,64,4384]{2,1,0:T(8,128)(2,1)S(1)} collective-permute-done((bf16[1,64,4384]{2,1,0:T(8,128)(2,1)S(1)}, bf16[1,64,4384]{2,1,0:T(8,128)(2,1)S(1)}, u32[]{:S(2)}, u32[]{:S(2)}) %collective-permute-start.3) | collective-permute-done | bytes 561184 | tf_op jit(solution)/shard_map/ppermute | solution.py:16
  45.5 12.8 %collective-permute-done.4 = bf16[1,64,4384]{2,1,0:T(8,128)(2,1)S(1)} collective-permute-done((bf16[1,64,4384]{2,1,0:T(8,128)(2,1)S(1)}, bf16[1,64,4384]{2,1,0:T(8,128)(2,1)S(1)}, u32[]{:S(2)}, u32[]{:S(2)}) %collective-permute-start.4) | collective-permute-done | bytes 561184 | tf_op jit(solution)/shard_map/ppermute | solution.py:16
  59.8 4.6 collective-permute-start.12
  64.4 7.9 collective-permute-done.5
  74.0 4.5 collective-permute-start.13
  78.5 11.4 collective-permute-done.6
  95.1 6.7 collective-permute-done.7
  102.4 4.8 collective-permute-start.15
  107.2 6.7 collective-permute-done.8
  118.2 5.5 collective-permute-start.16
  169.6 7.8 dynamic-slice_bitcast_fusion.1
  182.0 189.3 %while.61 = (s32[]{:T(128)}, bf16[64,1024]{1,0:T(8,128)(2,1)S(1)}, bf16[4,64,1024]{2,1,0:T(8,128)(2,1)}, bf16[4,64,1024]{2,1,0:T(8,128)(2,1)}, f32[4,64,4384]{2,...) while((s32[]{:T(128)}, bf16[64,1024]{1,0:T(8,128)(2,1)S(1)}, ...), condition=%wide.region_4.5_spmd, body=%wide.region_0.4_spmd.sunk | while | flops 1205211648 | bytes 37600076 | solution.py:160
  185.8 6.4 bitcast_dynamic-update-slice_fusion.17
  232.7 6.4 bitcast_dynamic-update-slice_fusion.17
  280.1 6.4 bitcast_dynamic-update-slice_fusion.17
  327.5 6.4 bitcast_dynamic-update-slice_fusion.17
  375.9 528.0 %while.62 = (s32[]{:T(128)}, bf16[64,1024]{1,0:T(8,128)(2,1)S(1)}, f32[1024]{0:T(1024)}, f32[4,2304]{1,0:T(4,128)}, f32[2304]{0:T(1024)}, /*index=5*/f32[32]{0:T...) while((s32[]{:T(128)}, bf16[64,1024]{1,0:T(8,128)(2,1)S(1)}, ...), condition=%wide.region_29.30_spmd.clone, body=%wide.region_5.29_spmd.clone.sunk | while | flops 1929479168 | bytes 86325424 | solution.py:220
  455.3 4.5 multiply_reduce_fusion.27
  459.8 5.0 fusion.300
  501.1 6.8 fusion.305
  585.0 5.0 fusion.300
  626.3 6.8 fusion.305
  712.4 5.0 fusion.300
  753.7 6.8 fusion.305
  839.8 5.0 fusion.300
  881.0 6.8 fusion.305
  903.9 6.0 convolution_bitcast_fusion.6
  910.2 9.5 convolution_bitcast_fusion.5
  919.8 73.1 %all-reduce.24 = (f32[1,1024]{1,0:T(1,128)}, f32[1,4,2304]{2,1,0:T(4,128)}, f32[1,2304]{1,0:T(1,128)}, f32[1,32]{1,0:T(1,128)}, f32[1,32]{1,0:T(1,128)}, /*index=5*/f32[1,32]{1,0:T(1,128)}, f32[1,2048]{1,0:T(1,128)}) all-reduce(f32[1,1024]{1,0:T(1,128)S(1)} %bitcast.405, ...), channel_id=1, replica_groups=mesh['section'=2,'dp'=16] {'dp'}, use_global_device_ids=true, to_apply=%region_32.33 | all-reduce | flops 14688 | bytes 117504 | tf_op jit(solution)/shard_map/psum | solution.py:233
  994.2 37.7 %reduce-scatter.5.cloned.1.call-done = f32[128,1024]{1,0:T(8,128)} async-done(((f32[2048,1024]{1,0:T(8,128)}), f32[128,1024]{1,0:T(8,128)}) %reduce-scatter.5.cloned.1.call-update) | async-done | bytes 524304 | tf_op jit(solution)/shard_map/reduce_scatter | solution.py:230
  1031.8 194.0 %reduce-scatter.3.cloned.1.call-done = f32[64,4384]{1,0:T(8,128)} async-done(((f32[1024,4384]{1,0:T(8,128)}), f32[64,4384]{1,0:T(8,128)}) %reduce-scatter.3.cloned.1.call-update) | async-done | bytes 1122320 | tf_op jit(solution)/shard_map/reduce_scatter | solution.py:227
  (904 shorter events, 683.5 us)
Async XLA Ops:
  7.2 153.4 %copy-start.10 = (bf16[1,64,4384]{2,1,0:T(8,128)(2,1)S(1)}, bf16[1,64,4384]{2,1,0:T(8,128)(2,1)}, u32[]{:S(2)}) copy-start(bf16[1,64,4384]{2,1,0:T(8,128)(2,1)} %param.19) | copy-start | bytes 1683460
  7.2 170.3 %all-gather.3.cloned.1.call-start = ((), (), s32[]{:S(2)}) async-start(), calls=%async_computation.2 | async-start | bytes 4456448 | tf_op jit(solution)/shard_map/all_gather | solution.py:137
  7.9 363.4 %all-gather.5.cloned.1.call-start = ((), (), s32[]{:S(2)}) async-start(), calls=%async_computation.3 | async-start | bytes 9748480 | tf_op jit(solution)/shard_map/all_gather | solution.py:164
  8.0 13.1 %collective-permute-start.2 = (bf16[1,64,4384]{2,1,0:T(8,128)(2,1)}, bf16[1,64,4384]{2,1,0:T(8,128)(2,1)S(1)}, u32[]{:S(2)}, u32[]{:S(2)}) collective-permute-start(bf16[1,64,4384]{2,1,0:T(8,128)(2,1)} %param.19), channel_id=1, source_target_pairs={{0,1},{1,2},{2,3},{3,4},{4,5},{5,6},{6,7},{7,8},{8,9},{9,10},{10,1... | collective-permute-start | bytes 1683464 | tf_op jit(solution)/shard_map/ppermute | solution.py:16
  21.1 19.9 %collective-permute-start.3 = (bf16[1,64,4384]{2,1,0:T(8,128)(2,1)S(1)}, bf16[1,64,4384]{2,1,0:T(8,128)(2,1)S(1)}, u32[]{:S(2)}, u32[]{:S(2)}) collective-permute-start(bf16[1,64,4384]{2,1,0:T(8,128)(2,1)S(1)} %collective-permute-done.2), channel_id=1, source_target_pairs={{0,1},{1,2},{2,3},{3,4},{4,5},{5,6},{6,7},{7,8},{8,9},{9,10},{10,1... | collective-permute-start | bytes 1683464 | tf_op jit(solution)/shard_map/ppermute | solution.py:16
  21.1 19.9 %collective-permute-start.10 = (bf16[1,64,4384]{2,1,0:T(8,128)(2,1)}, bf16[1,64,4384]{2,1,0:T(8,128)(2,1)S(1)}, u32[]{:S(2)}, u32[]{:S(2)}) collective-permute-start(bf16[1,64,4384]{2,1,0:T(8,128)(2,1)} %param.19), channel_id=1, source_target_pairs={{0,15},{1,0},{2,1},{3,2},{4,3},{5,4},{6,5},{7,6},{8,7},{9,8},{10,9... | collective-permute-start | bytes 1683464 | tf_op jit(solution)/shard_map/ppermute | solution.py:18
  41.0 17.3 %collective-permute-start.4 = (bf16[1,64,4384]{2,1,0:T(8,128)(2,1)S(1)}, bf16[1,64,4384]{2,1,0:T(8,128)(2,1)S(1)}, u32[]{:S(2)}, u32[]{:S(2)}) collective-permute-start(bf16[1,64,4384]{2,1,0:T(8,128)(2,1)S(1)} %collective-permute-done.3), channel_id=1, source_target_pairs={{0,1},{1,2},{2,3},{3,4},{4,5},{5,6},{6,7},{7,8},{8,9},{9,10},{10,1... | collective-permute-start | bytes 1683464 | tf_op jit(solution)/shard_map/ppermute | solution.py:16
  41.0 18.8 %collective-permute-start.11 = (bf16[1,64,4384]{2,1,0:T(8,128)(2,1)S(1)}, bf16[1,64,4384]{2,1,0:T(8,128)(2,1)S(1)}, u32[]{:S(2)}, u32[]{:S(2)}) collective-permute-start(bf16[1,64,4384]{2,1,0:T(8,128)(2,1)S(1)} %collective-permute-done.10), channel_id=1, source_target_pairs={{0,15},{1,0},{2,1},{3,2},{4,3},{5,4},{6,5},{7,6},{8,7},{9,8},{10,9... | collective-permute-start | bytes 1683464 | tf_op jit(solution)/shard_map/ppermute | solution.py:18
  58.3 14.0 %collective-permute-start.5 = (bf16[1,64,4384]{2,1,0:T(8,128)(2,1)S(1)}, bf16[1,64,4384]{2,1,0:T(8,128)(2,1)S(1)}, u32[]{:S(2)}, u32[]{:S(2)}) collective-permute-start(bf16[1,64,4384]{2,1,0:T(8,128)(2,1)S(1)} %collective-permute-done.4), channel_id=1, source_target_pairs={{0,1},{1,2},{2,3},{3,4},{4,5},{5,6},{6,7},{7,8},{8,9},{9,10},{10,1... | collective-permute-start | bytes 1683464 | tf_op jit(solution)/shard_map/ppermute | solution.py:16
  59.8 13.4 %collective-permute-start.12 = (bf16[1,64,4384]{2,1,0:T(8,128)(2,1)S(1)}, bf16[1,64,4384]{2,1,0:T(8,128)(2,1)S(1)}, u32[]{:S(2)}, u32[]{:S(2)}) collective-permute-start(bf16[1,64,4384]{2,1,0:T(8,128)(2,1)S(1)} %collective-permute-done.11), channel_id=1, source_target_pairs={{0,15},{1,0},{2,1},{3,2},{4,3},{5,4},{6,5},{7,6},{8,7},{9,8},{10,9... | collective-permute-start | bytes 1683464 | tf_op jit(solution)/shard_map/ppermute | solution.py:18
  72.3 17.6 %collective-permute-start.6 = (bf16[1,64,4384]{2,1,0:T(8,128)(2,1)S(1)}, bf16[1,64,4384]{2,1,0:T(8,128)(2,1)S(1)}, u32[]{:S(2)}, u32[]{:S(2)}) collective-permute-start(bf16[1,64,4384]{2,1,0:T(8,128)(2,1)S(1)} %collective-permute-done.5), channel_id=1, source_target_pairs={{0,1},{1,2},{2,3},{3,4},{4,5},{5,6},{6,7},{7,8},{8,9},{9,10},{10,1... | collective-permute-start | bytes 1683464 | tf_op jit(solution)/shard_map/ppermute | solution.py:16
  74.0 15.9 %collective-permute-start.13 = (bf16[1,64,4384]{2,1,0:T(8,128)(2,1)S(1)}, bf16[1,64,4384]{2,1,0:T(8,128)(2,1)S(1)}, u32[]{:S(2)}, u32[]{:S(2)}) collective-permute-start(bf16[1,64,4384]{2,1,0:T(8,128)(2,1)S(1)} %collective-permute-done.12), channel_id=1, source_target_pairs={{0,15},{1,0},{2,1},{3,2},{4,3},{5,4},{6,5},{7,6},{8,7},{9,8},{10,9... | collective-permute-start | bytes 1683464 | tf_op jit(solution)/shard_map/ppermute | solution.py:18
  89.9 11.9 collective-permute-start.7
  90.8 11.6 collective-permute-start.14
  101.8 12.0 collective-permute-start.8
  102.4 15.8 %collective-permute-start.15 = (bf16[1,64,4384]{2,1,0:T(8,128)(2,1)}, bf16[1,64,4384]{2,1,0:T(8,128)(2,1)}, u32[]{:S(2)}, u32[]{:S(2)}) collective-permute-start(bf16[1,64,4384]{2,1,0:T(8,128)(2,1)} %collective-permute-done.14), channel_id=1, source_target_pairs={{0,15},{1,0},{2,1},{3,2},{4,3},{5,4},{6,5},{7,6},{8,7},{9,8},{10,9... | collective-permute-start | bytes 1683464 | tf_op jit(solution)/shard_map/ppermute | solution.py:18
  113.9 13.3 %collective-permute-start.9 = (bf16[1,64,4384]{2,1,0:T(8,128)(2,1)}, bf16[1,64,4384]{2,1,0:T(8,128)(2,1)}, u32[]{:S(2)}, u32[]{:S(2)}) collective-permute-start(bf16[1,64,4384]{2,1,0:T(8,128)(2,1)} %collective-permute-done.8), channel_id=1, source_target_pairs={{0,1},{1,2},{2,3},{3,4},{4,5},{5,6},{6,7},{7,8},{8,9},{9,10},{10,1... | collective-permute-start | bytes 1683464 | tf_op jit(solution)/shard_map/ppermute | solution.py:16
  113.9 917.9 %reduce-scatter.5.cloned.1.call-start = ((), (), s32[]{:S(2)}) async-start(), calls=%async_computation.5 | async-start | bytes 8912896 | tf_op jit(solution)/shard_map/reduce_scatter | solution.py:230
  118.2 32.5 %collective-permute-start.16 = (bf16[1,64,4384]{2,1,0:T(8,128)(2,1)}, bf16[1,64,4384]{2,1,0:T(8,128)(2,1)S(1)}, u32[]{:S(2)}, u32[]{:S(2)}) collective-permute-start(bf16[1,64,4384]{2,1,0:T(8,128)(2,1)} %collective-permute-done.15), channel_id=1, source_target_pairs={{0,15},{1,0},{2,1},{3,2},{4,3},{5,4},{6,5},{7,6},{8,7},{9,8},{10,9... | collective-permute-start | bytes 1683464 | tf_op jit(solution)/shard_map/ppermute | solution.py:18
  222.8 6.3 collective-permute-start
  269.7 6.9 collective-permute-start
  317.0 6.9 collective-permute-start
  364.5 6.9 collective-permute-start
  509.7 11.9 collective-permute-start.1
  635.0 14.1 %collective-permute-start.1 = (bf16[64,1024]{1,0:T(8,128)(2,1)S(1)}, bf16[64,1024]{1,0:T(8,128)(2,1)S(1)}, u32[]{:S(2)}, u32[]{:S(2)}) collective-permute-start(bf16[64,1024]{1,0:T(8,128)(2,1)S(1)} %get-tuple-element.1942), channel_id=1, source_target_pairs={{16,0},{17,1},{18,2},{19,3},{20,4},{21,5},{22,6},{23,7},{24,8},{25... | collective-permute-start | bytes 393224 | tf_op jit(solution)/shard_map/while/body/eval_jaxpr/ppermute | solution.py:26
  652.4 54.0 %copy-start.3 = (f32[62,2304]{1,0:T(8,128)}, f32[62,2304]{1,0:T(8,128)S(1)}, u32[]{:S(2)}) copy-start(f32[62,2304]{1,0:T(8,128)S(1)} %slice.394) | copy-start | bytes 1714180 | tf_op jit(solution)/shard_map/while
  762.3 14.0 %collective-permute-start.1 = (bf16[64,1024]{1,0:T(8,128)(2,1)S(1)}, bf16[64,1024]{1,0:T(8,128)(2,1)S(1)}, u32[]{:S(2)}, u32[]{:S(2)}) collective-permute-start(bf16[64,1024]{1,0:T(8,128)(2,1)S(1)} %get-tuple-element.1942), channel_id=1, source_target_pairs={{16,0},{17,1},{18,2},{19,3},{20,4},{21,5},{22,6},{23,7},{24,8},{25... | collective-permute-start | bytes 393224 | tf_op jit(solution)/shard_map/while/body/eval_jaxpr/ppermute | solution.py:26
  779.7 54.0 %copy-start.3 = (f32[62,2304]{1,0:T(8,128)}, f32[62,2304]{1,0:T(8,128)S(1)}, u32[]{:S(2)}) copy-start(f32[62,2304]{1,0:T(8,128)S(1)} %slice.394) | copy-start | bytes 1714180 | tf_op jit(solution)/shard_map/while
  889.6 14.1 %collective-permute-start.1 = (bf16[64,1024]{1,0:T(8,128)(2,1)S(1)}, bf16[64,1024]{1,0:T(8,128)(2,1)S(1)}, u32[]{:S(2)}, u32[]{:S(2)}) collective-permute-start(bf16[64,1024]{1,0:T(8,128)(2,1)S(1)} %get-tuple-element.1942), channel_id=1, source_target_pairs={{16,0},{17,1},{18,2},{19,3},{20,4},{21,5},{22,6},{23,7},{24,8},{25... | collective-permute-start | bytes 393224 | tf_op jit(solution)/shard_map/while/body/eval_jaxpr/ppermute | solution.py:26
  910.0 315.9 %reduce-scatter.3.cloned.1.call-start = ((), (), s32[]{:S(2)}) async-start(), calls=%async_computation.4 | async-start | bytes 19496960 | tf_op jit(solution)/shard_map/reduce_scatter | solution.py:227
  910.1 82.8 %copy-start.13 = (f32[4,64,1024]{2,1,0:T(8,128)S(1)}, f32[4,64,1024]{2,1,0:T(8,128)}, u32[]{:S(2)}) copy-start(f32[4,64,1024]{2,1,0:T(8,128)} %get-tuple-element.969) | copy-start | bytes 3145732
  910.1 82.8 %copy-start.14 = (f32[4,64,1024]{2,1,0:T(8,128)S(1)}, f32[4,64,1024]{2,1,0:T(8,128)}, u32[]{:S(2)}) copy-start(f32[4,64,1024]{2,1,0:T(8,128)} %get-tuple-element.964) | copy-start | bytes 3145732
  (114 other events, 1685.3 us)
Sparse Core Ops, SparseCore 0:
  10.2 74.6 all-gather.2
  114.0 91.6 all-gather.4
  910.1 121.6 reduce-scatter.4
  1036.5 189.3 reduce-scatter.2
